TPU v7x, 512 devices: a whole 4x8x8 slice. The times are simulated.
512 devices in a mesh: space: 64 (over y, z), orb: 8 (over x, core).
Axes of the slice: x: 4, y: 8, z: 8, core: 2. Of those that a mesh axis runs over, the one named last changes fastest.
Arguments:
- hamiltonian: bfloat16 [512, 7, 256, 256], P('space'), may hold values from -0.125 to 0.125
- orbitals: bfloat16 [256, 131072], P('orb', 'space'), may hold values from -6 to 6
- adjacency: int32 [512, 6], P('space'), may hold values from 0 to 511, as said below
Outputs:
- basis: float32 [256, 131072], P('orb', 'space')
- factor: float32 [256, 256], replicated
Inputs may be any that keep to these rules, and one draw needn't show every extreme that they name: `adjacency`: with elements in blocks of 8 (block b holds elements b * 8 to b * 8 + 7), face 0 of an element in block b lies in block b - 1 and face 1 in block b + 1 (both modulo the number of blocks), faces 2 to 5 in block b; for each face, the elements of a block name every element of the target block exactly once.
All inputs are finite; a program needn't handle non-finite values.
Results may differ from a plain program's by a relative error of at most 0.0041.
Values may be sent and summed in bfloat16 or wider, within the bound.
A program may use at most 64 MiB of HBM per device.

v0:
```python
import jax
import jax.numpy as jnp
from jax import lax
from jax.sharding import PartitionSpec as P

centre = 0.25
radius = 0.75


def with_halo(block, sides, width):
    for axis, dim in sides:
        count = lax.axis_size(axis)
        forward = [(i, i + 1) for i in range(count - 1)]
        forward.append((count - 1, 0))
        backward = [(target, source) for source, target in forward]
        low = lax.ppermute(
            lax.slice_in_dim(block, block.shape[dim] - width, None, axis=dim), axis, forward
        )
        high = lax.ppermute(lax.slice_in_dim(block, 0, width, axis=dim), axis, backward)
        block = jnp.concatenate([low, block, high], axis=dim)
    return block


def shards(hamiltonian, orbitals, adjacency):
    count = hamiltonian.shape[0]
    width = hamiltonian.shape[2]
    owned = orbitals.shape[0]
    total = count * lax.axis_size("space")
    first = lax.axis_index("space") * count
    located = (adjacency - first + count) % total

    def apply_ham(vec):
        padded = with_halo(vec, (("space", 1),), count * width)
        blocks = padded.reshape(owned, 3 * count, width)
        near = jnp.take(blocks, located.reshape(-1), axis=1).reshape(owned, count, 6, width)
        own_part = vec.reshape(owned, count, width)
        result = jnp.einsum(
            "oej,eij->oei", own_part, hamiltonian[:, 0], preferred_element_type=jnp.float32
        )
        result = result + jnp.einsum(
            "oefj,efij->oei", near, hamiltonian[:, 1:], preferred_element_type=jnp.float32
        )
        return result.reshape(owned, count * width)

    level_zero = orbitals.astype(jnp.float32)
    level_one = ((apply_ham(orbitals) - centre * level_zero) / radius).astype(jnp.bfloat16)
    one_wide = level_one.astype(jnp.float32)
    level_two = (2.0 * (apply_ham(level_one) - centre * one_wide) / radius - level_zero).astype(
        jnp.bfloat16
    )
    two_wide = level_two.astype(jnp.float32)
    filtered = 2.0 * (apply_ham(level_two) - centre * two_wide) / radius - one_wide
    row_piece = lax.all_to_all(filtered, "orb", split_axis=1, concat_axis=0, tiled=True)
    partial_gram = jnp.dot(row_piece, row_piece.T, precision=lax.Precision.HIGHEST)
    gram = lax.psum(partial_gram, ("space", "orb"))
    lower = jnp.linalg.cholesky(gram)
    solved = lax.linalg.triangular_solve(lower, row_piece, left_side=True, lower=True)
    basis = lax.all_to_all(solved, "orb", split_axis=0, concat_axis=1, tiled=True)
    return (basis, lower.T)


def solution(mesh):
    in_specs = (P("space", None, None, None), P("orb", "space"), P("space", None))
    out_specs = (P("orb", "space"), P())
    return jax.shard_map(shards, mesh=mesh, in_specs=in_specs, out_specs=out_specs, check_vma=False)
```

profile of v0, /device:TPU:24, one launch (start us, length us, event | category | flops | bytes accessed | tf_op | source)
XLA Modules:
  0.0 435.6 jit_solution(6208198198700955853)
XLA Ops:
  7.2 4.4 %collective-permute-start = (bf16[32,2048]{1,0:T(8,128)(2,1)}, bf16[32,2048]{1,0:T(8,128)(2,1)S(1)}, u32[]{:S(2)}, u32[]{:S(2)}) collective-permute-start(bf16[32,2048]{1,0:T(8,128)(2,1)} %param.6), channel_id=1, source_target_pairs={{0,8},{8,16},{16,24},{24,32},{32,40},{40,48},{48,56},{56,64},{64,7... | collective-permute-start | bytes 393224 | tf_op jit(solution)/shard_map/ppermute | solution.py:16
  11.6 8.5 %collective-permute-start.1 = (bf16[32,2048]{1,0:T(8,128)(2,1)}, bf16[32,2048]{1,0:T(8,128)(2,1)S(1)}, u32[]{:S(2)}, u32[]{:S(2)}) collective-permute-start(bf16[32,2048]{1,0:T(8,128)(2,1)} %param.6), channel_id=1, source_target_pairs={{8,0},{16,8},{24,16},{32,24},{40,32},{48,40},{56,48},{64,56},{72,6... | collective-permute-start | bytes 393224 | tf_op jit(solution)/shard_map/ppermute | solution.py:19
  24.9 4.7 %fusion.6 = f32[32,8,256]{2,0,1:T(8,128)S(1)} fusion(bf16[32,8,6,256]{3,0,2,1:T(8,128)(2,1)S(1)} %bitcast.139, bf16[8,7,256,256]{3,2,1,0:T(8,128)(2,1)} %param.5), kind=kOutput, calls=%fused_computation.11 | convolution fusion | flops 201326592 | bytes 7340032 | tf_op jit(solution)/shard_map/oefj,efij->oei/dot_general | solution.py:40
  29.6 1.6 fusion.16
  31.3 1.9 collective-permute-start.2
  33.3 6.4 %collective-permute-start.3 = (bf16[32,2048]{1,0:T(8,128)(2,1)S(1)}, bf16[32,2048]{1,0:T(8,128)(2,1)S(1)}, u32[]{:S(2)}, u32[]{:S(2)}) collective-permute-start(bf16[32,2048]{1,0:T(8,128)(2,1)S(1)} %fusion.27), channel_id=1, source_target_pairs={{8,0},{16,8},{24,16},{32,24},{40,32},{48,40},{56,48},{64,56},{72,6... | collective-permute-start | bytes 393224 | tf_op jit(solution)/shard_map/ppermute | solution.py:19
  40.7 1.5 collective-permute-done.3
  43.0 4.7 %fusion.9 = f32[8,32,256]{2,1,0:T(8,128)S(1)} fusion(bf16[32,8,6,256]{3,0,2,1:T(8,128)(2,1)S(1)} %bitcast.140, bf16[8,7,256,256]{3,2,1,0:T(8,128)(2,1)} %param.5), kind=kOutput, calls=%fused_computation.12 | convolution fusion | flops 201326592 | bytes 7340032 | tf_op jit(solution)/shard_map/oefj,efij->oei/dot_general | solution.py:40
  47.7 1.7 fusion.18
  49.5 2.9 collective-permute-start.4
  52.4 5.5 %collective-permute-start.5 = (bf16[32,2048]{1,0:T(8,128)(2,1)S(1)}, bf16[32,2048]{1,0:T(8,128)(2,1)S(1)}, u32[]{:S(2)}, u32[]{:S(2)}) collective-permute-start(bf16[32,2048]{1,0:T(8,128)(2,1)S(1)} %fusion.28), channel_id=1, source_target_pairs={{8,0},{16,8},{24,16},{32,24},{40,32},{48,40},{56,48},{64,56},{72,6... | collective-permute-start | bytes 393224 | tf_op jit(solution)/shard_map/ppermute | solution.py:19
  58.9 1.5 collective-permute-done.5
  61.2 4.7 %fusion.12 = f32[8,32,256]{2,1,0:T(8,128)S(1)} fusion(bf16[32,8,6,256]{3,0,2,1:T(8,128)(2,1)S(1)} %bitcast.138, bf16[8,7,256,256]{3,2,1,0:T(8,128)(2,1)} %param.5), kind=kOutput, calls=%fused_computation.13 | convolution fusion | flops 201326592 | bytes 7340032 | tf_op jit(solution)/shard_map/oefj,efij->oei/dot_general | solution.py:40
  65.9 1.7 fusion.17
  68.4 4.3 all-to-all-start
  73.0 7.3 %all-to-all-done = f32[32,8,256]{2,0,1:T(8,128)S(1)} async-done(((f32[32,8,256]{2,0,1:T(8,128)}), f32[32,8,256]{2,0,1:T(8,128)S(1)}, u32[]{:S(2)}, u32[]{:S(2)}) %all-to-all-start) | async-done | bytes 262176 | tf_op jit(solution)/shard_map/all_to_all | solution.py:53
  81.4 271.7 %all-reduce.3.cloned.1.call-done = f32[256,256]{0,1:T(8,128)} async-done(((f32[256,256]{0,1:T(8,128)}), f32[256,256]{0,1:T(8,128)}) %all-reduce.3.cloned.1.call-update) | async-done | bytes 262160 | tf_op jit(solution)/shard_map/psum | solution.py:55
  355.2 11.7 %cholesky.50 = f32[128,128]{1,0:T(8,128)S(1)} custom-call(f32[128,128]{1,0:T(8,128)S(1)} %cholesky.118), custom_call_target="Cholesky" | custom-call | tf_op jit(solution)/shard_map/jit(cholesky)/cholesky | solution.py:56
  366.9 9.8 %custom-call.14 = f32[1,128,128]{1,2,0:T(8,128)S(1)} custom-call(f32[1,128,128]{2,1,0:T(8,128)S(1)} %get-tuple-element.34), custom_call_target="InvertDiagBlocksLowerTriangular" | custom-call | tf_op jit(solution)/shard_map/jit(cholesky)/cholesky | solution.py:56
  377.2 11.7 %cholesky.105 = f32[128,128]{1,0:T(8,128)S(1)} custom-call(f32[128,128]{1,0:T(8,128)S(1)} %convolution_subtract_fusion.1), custom_call_target="Cholesky" | custom-call | tf_op jit(solution)/shard_map/jit(cholesky)/cholesky | solution.py:56
  391.0 4.0 while.1
  395.0 19.7 %custom-call.15 = f32[2,128,128]{1,2,0:T(8,128)S(1)} custom-call(f32[2,128,128]{2,1,0:T(8,128)S(1)} %get-tuple-element.10), custom_call_target="InvertDiagBlocksLowerTriangular" | custom-call | tf_op jit(solution)/shard_map/triangular_solve | solution.py:57
  416.3 4.3 all-to-all-start.1
  421.4 6.7 %all-to-all-done.1 = f32[8,32,256]{2,1,0:T(8,128)S(1)} async-done(((f32[8,32,256]{2,1,0:T(8,128)}), f32[8,32,256]{2,1,0:T(8,128)S(1)}, u32[]{:S(2)}, u32[]{:S(2)}) %all-to-all-start.1) | async-done | bytes 262176 | tf_op jit(solution)/shard_map/all_to_all | solution.py:58
  (59 shorter events, 21.1 us)
Async XLA Ops:
  7.2 22.4 %copy-start = (bf16[32,2048]{1,0:T(8,128)(2,1)S(1)}, bf16[32,2048]{1,0:T(8,128)(2,1)}, u32[]{:S(2)}) copy-start(bf16[32,2048]{1,0:T(8,128)(2,1)} %param.6) | copy-start | bytes 393220
  7.2 14.7 %collective-permute-start = (bf16[32,2048]{1,0:T(8,128)(2,1)}, bf16[32,2048]{1,0:T(8,128)(2,1)S(1)}, u32[]{:S(2)}, u32[]{:S(2)}) collective-permute-start(bf16[32,2048]{1,0:T(8,128)(2,1)} %param.6), channel_id=1, source_target_pairs={{0,8},{8,16},{16,24},{24,32},{32,40},{40,48},{48,56},{56,64},{64,7... | collective-permute-start | bytes 393224 | tf_op jit(solution)/shard_map/ppermute | solution.py:16
  11.6 11.5 %collective-permute-start.1 = (bf16[32,2048]{1,0:T(8,128)(2,1)}, bf16[32,2048]{1,0:T(8,128)(2,1)S(1)}, u32[]{:S(2)}, u32[]{:S(2)}) collective-permute-start(bf16[32,2048]{1,0:T(8,128)(2,1)} %param.6), channel_id=1, source_target_pairs={{8,0},{16,8},{24,16},{32,24},{40,32},{48,40},{56,48},{64,56},{72,6... | collective-permute-start | bytes 393224 | tf_op jit(solution)/shard_map/ppermute | solution.py:19
  31.3 9.3 %collective-permute-start.2 = (bf16[32,2048]{1,0:T(8,128)(2,1)S(1)}, bf16[32,2048]{1,0:T(8,128)(2,1)S(1)}, u32[]{:S(2)}, u32[]{:S(2)}) collective-permute-start(bf16[32,2048]{1,0:T(8,128)(2,1)S(1)} %fusion.27), channel_id=1, source_target_pairs={{0,8},{8,16},{16,24},{24,32},{32,40},{40,48},{48,56},{56,64},{64,7... | collective-permute-start | bytes 393224 | tf_op jit(solution)/shard_map/ppermute | solution.py:16
  33.3 8.9 %collective-permute-start.3 = (bf16[32,2048]{1,0:T(8,128)(2,1)S(1)}, bf16[32,2048]{1,0:T(8,128)(2,1)S(1)}, u32[]{:S(2)}, u32[]{:S(2)}) collective-permute-start(bf16[32,2048]{1,0:T(8,128)(2,1)S(1)} %fusion.27), channel_id=1, source_target_pairs={{8,0},{16,8},{24,16},{32,24},{40,32},{48,40},{56,48},{64,56},{72,6... | collective-permute-start | bytes 393224 | tf_op jit(solution)/shard_map/ppermute | solution.py:19
  49.5 9.4 %collective-permute-start.4 = (bf16[32,2048]{1,0:T(8,128)(2,1)S(1)}, bf16[32,2048]{1,0:T(8,128)(2,1)S(1)}, u32[]{:S(2)}, u32[]{:S(2)}) collective-permute-start(bf16[32,2048]{1,0:T(8,128)(2,1)S(1)} %fusion.28), channel_id=1, source_target_pairs={{0,8},{8,16},{16,24},{24,32},{32,40},{40,48},{48,56},{56,64},{64,7... | collective-permute-start | bytes 393224 | tf_op jit(solution)/shard_map/ppermute | solution.py:16
  52.4 8.0 %collective-permute-start.5 = (bf16[32,2048]{1,0:T(8,128)(2,1)S(1)}, bf16[32,2048]{1,0:T(8,128)(2,1)S(1)}, u32[]{:S(2)}, u32[]{:S(2)}) collective-permute-start(bf16[32,2048]{1,0:T(8,128)(2,1)S(1)} %fusion.28), channel_id=1, source_target_pairs={{8,0},{16,8},{24,16},{32,24},{40,32},{48,40},{56,48},{64,56},{72,6... | collective-permute-start | bytes 393224 | tf_op jit(solution)/shard_map/ppermute | solution.py:19
  68.4 11.8 %all-to-all-start = ((f32[32,8,256]{2,0,1:T(8,128)}), f32[32,8,256]{2,0,1:T(8,128)S(1)}, u32[]{:S(2)}, u32[]{:S(2)}) async-start(f32[32,8,256]{2,0,1:T(8,128)} %bitcast.115), calls=%async_computation | async-start | bytes 524288 | tf_op jit(solution)/shard_map/all_to_all | solution.py:53
  72.7 280.4 %all-reduce.3.cloned.1.call-start = ((), (), s32[]{:S(2)}) async-start(), calls=%async_computation.2 | async-start | bytes 524288 | tf_op jit(solution)/shard_map/psum | solution.py:55
  416.3 11.8 %all-to-all-start.1 = ((f32[8,32,256]{2,1,0:T(8,128)}), f32[8,32,256]{2,1,0:T(8,128)S(1)}, u32[]{:S(2)}, u32[]{:S(2)}) async-start(f32[8,32,256]{2,1,0:T(8,128)} %bitcast.26), calls=%async_computation.1 | async-start | bytes 524288 | tf_op jit(solution)/shard_map/all_to_all | solution.py:58
Sparse Core Ops, SparseCore 0:
  81.5 271.5 all-reduce.2
where the time goes:
time: 436 us
  waiting for transfers between devices  293 us (67%)
  other arithmetic  57.7 us (13%)
  starting transfers between devices  38.4 us (9%)
  matrix products  21.5 us (5%)
  between operations  15.6 us (4%)
  local copies, waits for them, and re-layouts  9.42 us (2%)
    psum x1, waiting for transfers between devices, shards(): gram = lax.psum(partial_gram, ('space', 'orb'))  272 us
    another operation x6, other arithmetic, shards(): lower = jnp.linalg.cholesky(gram)  33.9 us
    another operation x3, other arithmetic, shards(): lax.linalg.triangular_solve(lower, row_piece, left_side=True, lower=True)  20.4 us
    ppermute x3, starting transfers between devices, with_halo(): lax.ppermute(lax.slice_in_dim(block, 0, width, axis=dim), axis, backward)  20.3 us
    dot_general x3, matrix products, apply_ham(): jnp.einsum('oefj,efij->oei', near, hamiltonian[:, 1:], preferred_element_...  14.1 us
    ppermute x3, starting transfers between devices, with_halo(): lax.ppermute(lax.slice_in_dim(block, block.shape[dim] - width, None, axis...  9.26 us
  transfers between devices with their start and end apart: 9, of which 9 were waited for; matrix products, arithmetic and copies ran while one was open for 0% of the time, Pallas kernels for 0%

commit v1 on v0

--- a/solution.py
+++ b/solution.py
@@ -52,7 +52,7 @@
     filtered = 2.0 * (apply_ham(level_two) - centre * two_wide) / radius - one_wide
     row_piece = lax.all_to_all(filtered, "orb", split_axis=1, concat_axis=0, tiled=True)
     partial_gram = jnp.dot(row_piece, row_piece.T, precision=lax.Precision.HIGHEST)
-    gram = lax.psum(partial_gram, ("space", "orb"))
+    gram = lax.psum(lax.psum(partial_gram, "space"), "orb")
     lower = jnp.linalg.cholesky(gram)
     solved = lax.linalg.triangular_solve(lower, row_piece, left_side=True, lower=True)
     basis = lax.all_to_all(solved, "orb", split_axis=0, concat_axis=1, tiled=True)

time: 436 us -> 387 us (0.89)
  the two profiles are of different devices: /device:TPU:24 before, /device:TPU:1 now
where the time goes in v1:
time: 387 us; the launch traced here: 386 us
  waiting for transfers between devices  228 us (59%)
  other arithmetic  57.7 us (15%)
  starting transfers between devices  40.2 us (10%)
  matrix products  21.5 us (6%)
  between operations  15.6 us (4%)
  blocking collectives  14.1 us (4%)
  local copies, waits for them, and re-layouts  8.71 us (2%)
    psum x2, waiting for transfers between devices, shards(): gram = lax.psum(lax.psum(partial_gram, 'space'), 'orb')  217 us
    another operation x6, other arithmetic, shards(): lower = jnp.linalg.cholesky(gram)  33.9 us
    ppermute x3, starting transfers between devices, with_halo(): lax.ppermute(lax.slice_in_dim(block, 0, width, axis=dim), axis, backward)  25.9 us
    another operation x3, other arithmetic, shards(): lax.linalg.triangular_solve(lower, row_piece, left_side=True, lower=True)  20.4 us
    dot_general x3, matrix products, apply_ham(): jnp.einsum('oefj,efij->oei', near, hamiltonian[:, 1:], preferred_element_...  14.1 us
    all_to_all x1, blocking collectives, shards(): lax.all_to_all(filtered, 'orb', split_axis=1, concat_axis=0, tiled=True)  14.1 us
    ppermute x3, starting transfers between devices, with_halo(): lax.ppermute(lax.slice_in_dim(block, block.shape[dim] - width, None, axis...  8.66 us
  transfers between devices with their start and end apart: 9, of which 9 were waited for; matrix products, arithmetic and copies ran while one was open for 0% of the time, Pallas kernels for 0%

profile of v1, /device:TPU:1, one launch (start us, length us, event | category | flops | bytes accessed | tf_op | source)
XLA Modules:
  0.0 385.9 jit_solution(13405184036159546715)
XLA Ops:
  7.2 4.8 %collective-permute-start = (bf16[32,2048]{1,0:T(8,128)(2,1)}, bf16[32,2048]{1,0:T(8,128)(2,1)S(1)}, u32[]{:S(2)}, u32[]{:S(2)}) collective-permute-start(bf16[32,2048]{1,0:T(8,128)(2,1)} %param.6), channel_id=1, source_target_pairs={{0,8},{8,16},{16,24},{24,32},{32,40},{40,48},{48,56},{56,64},{64,7... | collective-permute-start | bytes 393224 | tf_op jit(solution)/shard_map/ppermute | solution.py:16
  12.0 11.5 %collective-permute-start.1 = (bf16[32,2048]{1,0:T(8,128)(2,1)}, bf16[32,2048]{1,0:T(8,128)(2,1)S(1)}, u32[]{:S(2)}, u32[]{:S(2)}) collective-permute-start(bf16[32,2048]{1,0:T(8,128)(2,1)} %param.6), channel_id=1, source_target_pairs={{8,0},{16,8},{24,16},{32,24},{40,32},{48,40},{56,48},{64,56},{72,6... | collective-permute-start | bytes 393224 | tf_op jit(solution)/shard_map/ppermute | solution.py:19
  27.8 4.7 %fusion.6 = f32[32,8,256]{2,0,1:T(8,128)S(1)} fusion(bf16[32,8,6,256]{3,0,2,1:T(8,128)(2,1)S(1)} %bitcast.140, bf16[8,7,256,256]{3,2,1,0:T(8,128)(2,1)} %param.5), kind=kOutput, calls=%fused_computation.11 | convolution fusion | flops 201326592 | bytes 7340032 | tf_op jit(solution)/shard_map/oefj,efij->oei/dot_general | solution.py:40
  32.5 1.6 fusion.16
  34.2 1.9 collective-permute-start.2
  36.2 7.3 %collective-permute-start.3 = (bf16[32,2048]{1,0:T(8,128)(2,1)S(1)}, bf16[32,2048]{1,0:T(8,128)(2,1)S(1)}, u32[]{:S(2)}, u32[]{:S(2)}) collective-permute-start(bf16[32,2048]{1,0:T(8,128)(2,1)S(1)} %fusion.27), channel_id=1, source_target_pairs={{8,0},{16,8},{24,16},{32,24},{40,32},{48,40},{56,48},{64,56},{72,6... | collective-permute-start | bytes 393224 | tf_op jit(solution)/shard_map/ppermute | solution.py:19
  43.9 1.5 collective-permute-done.3
  46.3 4.7 %fusion.9 = f32[8,32,256]{2,1,0:T(8,128)S(1)} fusion(bf16[32,8,6,256]{3,0,2,1:T(8,128)(2,1)S(1)} %bitcast.141, bf16[8,7,256,256]{3,2,1,0:T(8,128)(2,1)} %param.5), kind=kOutput, calls=%fused_computation.12 | convolution fusion | flops 201326592 | bytes 7340032 | tf_op jit(solution)/shard_map/oefj,efij->oei/dot_general | solution.py:40
  51.0 1.7 fusion.18
  52.7 1.9 collective-permute-start.4
  54.7 7.1 %collective-permute-start.5 = (bf16[32,2048]{1,0:T(8,128)(2,1)S(1)}, bf16[32,2048]{1,0:T(8,128)(2,1)S(1)}, u32[]{:S(2)}, u32[]{:S(2)}) collective-permute-start(bf16[32,2048]{1,0:T(8,128)(2,1)S(1)} %fusion.28), channel_id=1, source_target_pairs={{8,0},{16,8},{24,16},{32,24},{40,32},{48,40},{56,48},{64,56},{72,6... | collective-permute-start | bytes 393224 | tf_op jit(solution)/shard_map/ppermute | solution.py:19
  62.2 1.5 collective-permute-done.5
  64.6 4.7 %fusion.12 = f32[8,32,256]{2,1,0:T(8,128)S(1)} fusion(bf16[32,8,6,256]{3,0,2,1:T(8,128)(2,1)S(1)} %bitcast.139, bf16[8,7,256,256]{3,2,1,0:T(8,128)(2,1)} %param.5), kind=kOutput, calls=%fused_computation.13 | convolution fusion | flops 201326592 | bytes 7340032 | tf_op jit(solution)/shard_map/oefj,efij->oei/dot_general | solution.py:40
  69.3 1.7 fusion.17
  71.0 14.1 %all_to_all.38 = f32[32,8,256]{2,0,1:T(8,128)S(1)} all-to-all(f32[32,8,256]{2,0,1:T(8,128)S(1)} %bitcast.138), channel_id=1, replica_groups=mesh['space'=64,'orb'=8] {'orb'}, dimensions={1} | all-to-all | bytes 524288 | tf_op jit(solution)/shard_map/all_to_all | solution.py:53
  86.5 144.1 %all-reduce.4.cloned.1.call-done = f32[256,256]{0,1:T(8,128)} async-done(((f32[256,256]{0,1:T(8,128)}), f32[256,256]{0,1:T(8,128)}) %all-reduce.4.cloned.1.call-update) | async-done | bytes 262160 | tf_op jit(solution)/shard_map/psum | solution.py:55
  230.7 72.6 %all-reduce.6.cloned.1.call-done = f32[256,256]{0,1:T(8,128)} async-done(((f32[256,256]{0,1:T(8,128)}), f32[256,256]{0,1:T(8,128)}) %all-reduce.6.cloned.1.call-update) | async-done | bytes 262160 | tf_op jit(solution)/shard_map/psum | solution.py:55
  305.4 11.7 %cholesky.50 = f32[128,128]{1,0:T(8,128)S(1)} custom-call(f32[128,128]{1,0:T(8,128)S(1)} %cholesky.118), custom_call_target="Cholesky" | custom-call | tf_op jit(solution)/shard_map/jit(cholesky)/cholesky | solution.py:56
  317.2 9.8 %custom-call.14 = f32[1,128,128]{1,2,0:T(8,128)S(1)} custom-call(f32[1,128,128]{2,1,0:T(8,128)S(1)} %get-tuple-element.34), custom_call_target="InvertDiagBlocksLowerTriangular" | custom-call | tf_op jit(solution)/shard_map/jit(cholesky)/cholesky | solution.py:56
  327.4 11.7 %cholesky.105 = f32[128,128]{1,0:T(8,128)S(1)} custom-call(f32[128,128]{1,0:T(8,128)S(1)} %convolution_subtract_fusion.1), custom_call_target="Cholesky" | custom-call | tf_op jit(solution)/shard_map/jit(cholesky)/cholesky | solution.py:56
  341.2 4.0 %while.1 = (s32[]{:T(128)}, f32[256,256]{1,0:T(8,128)S(1)}, s32[2,2]{1,0:T(2,128)S(1)}, f32[2,128,128]{2,1,0:T(8,128)S(1)}, s32[]{:T(128)}) while((s32[]{:T(128)}, f32[256,256]{1,0:T(8,128)S(1)}, s32[2,2]{1,0:T(2,128)S(1)}, f32[2,128,128]{2,1,0:T(8,128)S(1)}, s32[]{:T(128)}) %tuple.33), condition=%wide.while_cond, body=%wide.while_body.sunk | while | flops 2 | bytes 131181 | solution.py:57
  345.2 19.7 %custom-call.15 = f32[2,128,128]{1,2,0:T(8,128)S(1)} custom-call(f32[2,128,128]{2,1,0:T(8,128)S(1)} %get-tuple-element.10), custom_call_target="InvertDiagBlocksLowerTriangular" | custom-call | tf_op jit(solution)/shard_map/triangular_solve | solution.py:57
  366.5 5.4 %all-to-all-start.1 = ((f32[8,32,256]{2,1,0:T(8,128)}), f32[8,32,256]{2,1,0:T(8,128)S(1)}, u32[]{:S(2)}, u32[]{:S(2)}) async-start(f32[8,32,256]{2,1,0:T(8,128)} %bitcast.26), calls=%async_computation.1 | async-start | bytes 524288 | tf_op jit(solution)/shard_map/all_to_all | solution.py:58
  372.7 5.7 %all-to-all-done.1 = f32[8,32,256]{2,1,0:T(8,128)S(1)} async-done(((f32[8,32,256]{2,1,0:T(8,128)}), f32[8,32,256]{2,1,0:T(8,128)S(1)}, u32[]{:S(2)}, u32[]{:S(2)}) %all-to-all-start.1) | async-done | bytes 262176 | tf_op jit(solution)/shard_map/all_to_all | solution.py:58
  (61 shorter events, 18.7 us)
Async XLA Ops:
  7.2 25.3 %copy-start = (bf16[32,2048]{1,0:T(8,128)(2,1)S(1)}, bf16[32,2048]{1,0:T(8,128)(2,1)}, u32[]{:S(2)}) copy-start(bf16[32,2048]{1,0:T(8,128)(2,1)} %param.6) | copy-start | bytes 393220
  7.2 223.4 %all-reduce.4.cloned.1.call-start = ((), (), s32[]{:S(2)}) async-start(), calls=%async_computation.2 | async-start | bytes 524288 | tf_op jit(solution)/shard_map/psum | solution.py:55
  7.2 17.8 %collective-permute-start = (bf16[32,2048]{1,0:T(8,128)(2,1)}, bf16[32,2048]{1,0:T(8,128)(2,1)S(1)}, u32[]{:S(2)}, u32[]{:S(2)}) collective-permute-start(bf16[32,2048]{1,0:T(8,128)(2,1)} %param.6), channel_id=1, source_target_pairs={{0,8},{8,16},{16,24},{24,32},{32,40},{40,48},{48,56},{56,64},{64,7... | collective-permute-start | bytes 393224 | tf_op jit(solution)/shard_map/ppermute | solution.py:16
  12.0 14.0 %collective-permute-start.1 = (bf16[32,2048]{1,0:T(8,128)(2,1)}, bf16[32,2048]{1,0:T(8,128)(2,1)S(1)}, u32[]{:S(2)}, u32[]{:S(2)}) collective-permute-start(bf16[32,2048]{1,0:T(8,128)(2,1)} %param.6), channel_id=1, source_target_pairs={{8,0},{16,8},{24,16},{32,24},{40,32},{48,40},{56,48},{64,56},{72,6... | collective-permute-start | bytes 393224 | tf_op jit(solution)/shard_map/ppermute | solution.py:19
  34.2 9.7 %collective-permute-start.2 = (bf16[32,2048]{1,0:T(8,128)(2,1)S(1)}, bf16[32,2048]{1,0:T(8,128)(2,1)S(1)}, u32[]{:S(2)}, u32[]{:S(2)}) collective-permute-start(bf16[32,2048]{1,0:T(8,128)(2,1)S(1)} %fusion.27), channel_id=1, source_target_pairs={{0,8},{8,16},{16,24},{24,32},{32,40},{40,48},{48,56},{56,64},{64,7... | collective-permute-start | bytes 393224 | tf_op jit(solution)/shard_map/ppermute | solution.py:16
  36.2 9.3 %collective-permute-start.3 = (bf16[32,2048]{1,0:T(8,128)(2,1)S(1)}, bf16[32,2048]{1,0:T(8,128)(2,1)S(1)}, u32[]{:S(2)}, u32[]{:S(2)}) collective-permute-start(bf16[32,2048]{1,0:T(8,128)(2,1)S(1)} %fusion.27), channel_id=1, source_target_pairs={{8,0},{16,8},{24,16},{32,24},{40,32},{48,40},{56,48},{64,56},{72,6... | collective-permute-start | bytes 393224 | tf_op jit(solution)/shard_map/ppermute | solution.py:19
  52.7 9.4 %collective-permute-start.4 = (bf16[32,2048]{1,0:T(8,128)(2,1)S(1)}, bf16[32,2048]{1,0:T(8,128)(2,1)S(1)}, u32[]{:S(2)}, u32[]{:S(2)}) collective-permute-start(bf16[32,2048]{1,0:T(8,128)(2,1)S(1)} %fusion.28), channel_id=1, source_target_pairs={{0,8},{8,16},{16,24},{24,32},{32,40},{40,48},{48,56},{56,64},{64,7... | collective-permute-start | bytes 393224 | tf_op jit(solution)/shard_map/ppermute | solution.py:16
  54.7 9.0 %collective-permute-start.5 = (bf16[32,2048]{1,0:T(8,128)(2,1)S(1)}, bf16[32,2048]{1,0:T(8,128)(2,1)S(1)}, u32[]{:S(2)}, u32[]{:S(2)}) collective-permute-start(bf16[32,2048]{1,0:T(8,128)(2,1)S(1)} %fusion.28), channel_id=1, source_target_pairs={{8,0},{16,8},{24,16},{32,24},{40,32},{48,40},{56,48},{64,56},{72,6... | collective-permute-start | bytes 393224 | tf_op jit(solution)/shard_map/ppermute | solution.py:19
  86.3 217.0 %all-reduce.6.cloned.1.call-start = ((), (), s32[]{:S(2)}) async-start(), calls=%async_computation.3 | async-start | bytes 524288 | tf_op jit(solution)/shard_map/psum | solution.py:55
  366.5 11.9 %all-to-all-start.1 = ((f32[8,32,256]{2,1,0:T(8,128)}), f32[8,32,256]{2,1,0:T(8,128)S(1)}, u32[]{:S(2)}, u32[]{:S(2)}) async-start(f32[8,32,256]{2,1,0:T(8,128)} %bitcast.26), calls=%async_computation.1 | async-start | bytes 524288 | tf_op jit(solution)/shard_map/all_to_all | solution.py:58
Sparse Core Ops, SparseCore 0:
  86.4 144.1 all-reduce.3
  232.9 70.3 all-reduce.5
